TPU v7x, 32 devices: a whole 2x2x4 slice. The times are simulated.
32 devices in a mesh: rep: 2 (over y), req: 4 (over z), mp: 4 (over x, core).
Axes of the slice: x: 2, y: 2, z: 4, core: 2. Of those that a mesh axis runs over, the one named last changes fastest.
Arguments:
- hidden_in: bfloat16 [128, 2, 8192], P(('rep', 'req'), None, 'mp'), parts along dimension 0, may hold values from -6 to 6
- frozen_query_rows: bfloat16 [128, 2, 8192], P(('rep', 'req'), None, 'mp'), parts along dimension 0, may hold values from -6 to 86
- new_kv: bfloat16 [128, 2, 2, 1024], P(('rep', 'req'), None, None, 'mp'), parts along dimension 0, may hold values from -6 to 31
- adapter_of: int32 [128], P(('rep', 'req')), parts along dimension 0, may hold values from 0 to 7, as said below
- adapter_home: int32 [16], P('rep'), parts along dimension 0, may hold values from 0 to 7, as said below
- a_store: bfloat16 [16, 64, 8192], P(('rep', 'req'), None, 'mp'), parts along dimension 0, may hold values from -0.0625 to 0.0625
- b_store: bfloat16 [16, 64, 8192], P(('rep', 'req'), None, 'mp'), parts along dimension 0, may hold values from -0.75 to 0.75
- kv_pool: bfloat16 [2, 1024, 16, 1024], P(None, ('rep', 'req'), None, 'mp'), parts along dimension 1, may hold values from -6 to 31
- page_table: int32 [128, 8], P(('rep', 'req')), parts along dimension 0, may hold values from 0 to 127, as said below
- cached_len: int32 [128], P(('rep', 'req')), parts along dimension 0, may hold values from 32 to 128
- new_group: int32 [128], P(('rep', 'req')), parts along dimension 0, may hold values from 0 to 3, as said below
Outputs:
- attended: bfloat16 [128, 2, 8192], P(('rep', 'req'), None, 'mp'), parts along dimension 0
- cache: bfloat16 [2, 128, 128, 1024], P(None, ('rep', 'req'), None, 'mp'), parts along dimension 1
There are 2 independent parts, one for each index of `rep`. A program takes and returns all parts, laid end to end along the dimension named above; each array names one. Nothing has to cross between parts.
Inputs may be any that keep to these rules, and one draw needn't show every extreme that they name: A permutation: adapter a lives in store slot adapter_home[a], which belongs to group adapter_home[a] div 2. `adapter_of`: the requests of one group (new rows h * 16 to h * 16 + 15) use adapters of min(16, number of groups) different owners, at most 4 requests an owner, a number reached in every group; all requests of one group whose adapters have one owner use the same adapter. `page_table`: the rows of one group name each of its 128 pages once. `new_group`: A request keeps its slot (row mod 16); the same 4 slots keep their group in every group; every group receives exactly one request into each slot; no group sends more than 3 requests to one other group, and some pair of groups reaches it.
All inputs are finite; a program needn't handle non-finite values.
Results may differ from a plain program's by a relative error of at most 0.0069.
Values may be sent and summed in bfloat16 or wider, within the bound.
A program may use at most 64 MiB of HBM per device.

v0:
```python
import jax
import jax.numpy as jnp
from jax import lax
from jax.sharding import PartitionSpec as P

HEAD = 128
NEG_FILL = -1e30


def attend(query_vectors, cached_keys, cached_values, length, fresh_kv):
    row_count, step_count, q_width = query_vectors.shape
    context = cached_keys.shape[1]
    kv_width = cached_keys.shape[2]
    kv_heads = kv_width // HEAD
    per_kv = q_width // kv_width
    score_scale = HEAD ** (-0.5)
    q_split = query_vectors.reshape(row_count, step_count, kv_heads, per_kv, HEAD)
    k_split = cached_keys.reshape(row_count, context, kv_heads, HEAD)
    v_split = cached_values.reshape(row_count, context, kv_heads, HEAD)
    new_keys = fresh_kv[:, :, 0].reshape(row_count, step_count, kv_heads, HEAD)
    new_values = fresh_kv[:, :, 1].reshape(row_count, step_count, kv_heads, HEAD)
    old_scores = (
        jnp.einsum("bskgd,bjkd->bskgj", q_split, k_split, preferred_element_type=jnp.float32)
        * score_scale
    )
    visible = jnp.arange(context)[None, :] < length[:, None]
    old_scores = jnp.where(visible[:, None, None, None, :], old_scores, NEG_FILL)
    new_scores = (
        jnp.einsum("bskgd,btkd->bskgt", q_split, new_keys, preferred_element_type=jnp.float32)
        * score_scale
    )
    causal = jnp.arange(step_count)[None, :] <= jnp.arange(step_count)[:, None]
    new_scores = jnp.where(causal[None, :, None, None, :], new_scores, NEG_FILL)
    scores = jnp.concatenate([old_scores, new_scores], axis=-1)
    row_max = jnp.max(scores, axis=-1, keepdims=True)
    weights = jnp.exp(scores - row_max)
    probabilities = (weights / jnp.sum(weights, axis=-1, keepdims=True)).astype(jnp.bfloat16)
    attention_out = jnp.einsum(
        "bskgj,bjkd->bskgd",
        probabilities[..., :context],
        v_split,
        preferred_element_type=jnp.float32,
    )
    attention_out = attention_out + jnp.einsum(
        "bskgt,btkd->bskgd",
        probabilities[..., context:],
        new_values,
        preferred_element_type=jnp.float32,
    )
    return attention_out.reshape(row_count, step_count, q_width).astype(jnp.bfloat16)


def adapter_rank_width(rank_partial_sum):
    return lax.psum(rank_partial_sum, "mp")


def per_device(
    hidden_in,
    frozen_query_rows,
    new_kv,
    adapter_of,
    adapter_home,
    a_store,
    b_store,
    kv_pool,
    page_table,
    cached_len,
    new_group,
):
    groups = lax.axis_size("req")
    my_group = lax.axis_index("req")
    per_group = adapter_of.shape[0]
    store_count = a_store.shape[0]
    context = page_table.shape[1] * kv_pool.shape[2]
    kv_width = kv_pool.shape[3]
    move_cap = -(-(per_group - per_group // 4) // groups)
    group_ids = jnp.arange(groups, dtype=jnp.int32)
    slot_ids = jnp.arange(per_group, dtype=jnp.int32)
    buffer_ids = jnp.arange(groups * move_cap, dtype=jnp.int32)
    adapter_slot = jnp.take(adapter_home, adapter_of)
    owners = adapter_slot // store_count
    local_pick = adapter_slot % store_count
    owner_hit = owners[:, None] == group_ids[None, :]
    wanted = jnp.max(jnp.where(owner_hit, local_pick[:, None], -1), axis=0)
    moving = new_group != my_group
    dest_hit = (new_group[:, None] == group_ids[None, :]) & moving[:, None]
    order_in = jnp.cumsum(dest_hit.astype(jnp.int32), axis=0) - 1
    position = jnp.sum(jnp.where(dest_hit, order_in, 0), axis=1)
    flat_slot = jnp.where(moving, new_group * move_cap + position, -1)
    slot_match = flat_slot[None, :] == buffer_ids[:, None]
    send_src = jnp.where(
        jnp.any(slot_match, axis=1),
        jnp.sum(jnp.where(slot_match, slot_ids[None, :], 0), axis=1),
        -1,
    )
    safe_src = jnp.maximum(send_src, 0)
    send_len = jnp.where(send_src >= 0, jnp.take(cached_len, safe_src), 0)
    got_wanted, got_slots, got_lens = (
        lax.all_to_all(wanted, "req", split_axis=0, concat_axis=0, tiled=True),
        lax.all_to_all(
            send_src.reshape(groups, move_cap), "req", split_axis=0, concat_axis=0, tiled=True
        ),
        lax.all_to_all(
            send_len.reshape(groups, move_cap), "req", split_axis=0, concat_axis=0, tiled=True
        ),
    )
    page_rows = jnp.take(kv_pool, page_table.reshape(-1), axis=1)
    cache_old = page_rows.reshape(2, per_group, context, kv_width)
    incoming = got_slots.reshape(-1)
    in_match = incoming[None, :] == slot_ids[:, None]
    in_index = jnp.sum(jnp.where(in_match, buffer_ids[None, :], 0), axis=1)
    len_new = jnp.where(moving, jnp.take(got_lens.reshape(-1), in_index), cached_len)
    wanted_slot = jnp.maximum(got_wanted, 0)
    a_panels, b_panels = (
        lax.all_to_all(
            jnp.take(a_store, wanted_slot, axis=0), "req", split_axis=0, concat_axis=0, tiled=True
        ),
        lax.all_to_all(
            jnp.take(b_store, wanted_slot, axis=0), "req", split_axis=0, concat_axis=0, tiled=True
        ),
    )
    a_rows = jnp.take(a_panels, owners, axis=0)
    up_panel_rows = jnp.take(b_panels, owners, axis=0)
    rank_slice_product = jnp.einsum(
        "rsd,rkd->rsk", hidden_in, a_rows, preferred_element_type=jnp.float32
    )
    complete_rank_product = adapter_rank_width(rank_slice_product).astype(jnp.bfloat16)
    adapter_query_delta = jnp.einsum(
        "gxj,gjv->gxv", complete_rank_product, up_panel_rows, preferred_element_type=jnp.float32
    )
    query_vectors = (frozen_query_rows.astype(jnp.float32) + adapter_query_delta).astype(
        jnp.bfloat16
    )
    far_cache = jnp.take(cache_old, safe_src, axis=1)
    send_pages = far_cache.reshape(2, groups, move_cap, context, kv_width)
    got_pages = lax.all_to_all(send_pages, "req", split_axis=1, concat_axis=1, tiled=True)
    pooled = jnp.concatenate(
        [cache_old, got_pages.reshape(2, groups * move_cap, context, kv_width)], axis=1
    )
    source = jnp.where(moving, per_group + in_index, slot_ids)
    cache_new = jnp.take(pooled, source, axis=1)
    attended = attend(query_vectors, cache_new[0], cache_new[1], len_new, new_kv)
    return (attended, cache_new)


def solution(mesh):
    placed = (
        P(("rep", "req"), None, "mp"),
        P(("rep", "req"), None, "mp"),
        P(("rep", "req"), None, None, "mp"),
        P(("rep", "req")),
        P("rep"),
        P(("rep", "req"), None, "mp"),
        P(("rep", "req"), None, "mp"),
        P(None, ("rep", "req"), None, "mp"),
        P(("rep", "req"), None),
        P(("rep", "req")),
        P(("rep", "req")),
    )
    return jax.shard_map(
        per_device,
        mesh=mesh,
        in_specs=placed,
        out_specs=(P(("rep", "req"), None, "mp"), P(None, ("rep", "req"), None, "mp")),
        check_vma=False,
    )
```

profile of v0, /device:TPU:0, one launch (start us, length us, event | category | flops | bytes accessed | tf_op | source)
XLA Modules:
  0.0 155.8 jit_solution(11224241576532435948)
XLA Ops:
  4.2 6.3 %all-to-all-start.3 = ((s32[4,1,1]{2,1,0:T(1,128)}), s32[4,1,1]{2,1,0:T(1,128)S(1)}, u32[]{:S(2)}, u32[]{:S(2)}) async-start(s32[4,1,1]{2,1,0:T(1,128)} %copy.112), calls=%async_computation.3 | async-start | bytes 4096 | tf_op jit(solution)/shard_map/all_to_all | solution.py:99
  17.1 5.1 %all-to-all-start = ((s32[4,1,3]{2,1,0:T(1,128)}), s32[4,1,3]{2,1,0:T(1,128)S(1)}, u32[]{:S(2)}, u32[]{:S(2)}) async-start(s32[4,1,3]{2,1,0:T(1,128)} %bitcast), calls=%async_computation | async-start | bytes 4096 | tf_op jit(solution)/shard_map/all_to_all | solution.py:100
  24.0 2.6 %gather_fusion.8 = bf16[4,64,2048]{2,1,0:T(8,128)(2,1)} fusion(bf16[2,64,2048]{2,1,0:T(8,128)(2,1)} %param.21, s32[1024]{0:T(1024)S(1)} %pad_clamp_fusion.1), kind=kCustom, calls=%fused_computation.2.clone | custom fusion | bytes 2097168 | tf_op jit(solution)/shard_map/jit(_take)/gather | solution.py:119
  27.6 4.1 %all-to-all-start.2 = ((s32[4,1,3]{2,1,0:T(1,128)}), s32[4,1,3]{2,1,0:T(1,128)S(1)}, u32[]{:S(2)}, u32[]{:S(2)}) async-start(s32[4,1,3]{2,1,0:T(1,128)} %bitcast.10), calls=%async_computation.2 | async-start | bytes 4096 | tf_op jit(solution)/shard_map/all_to_all | solution.py:103
  31.8 2.8 %broadcast_select_fusion.1 = (bf16[4,64,2048]{2,1,0:T(8,128)(2,1)}, bf16[4,64,2048]{2,1,0:T(8,128)(2,1)}) fusion(bf16[4,64,2048]{2,1,0:T(8,128)(2,1)S(1)} %gather_fusion.6, pred[4]{0:T(512)(128)(4,1)S(1)} %compare_and_fusion.2, bf16[4,64,2048]{2,1,0:T(8,128)(2,1)} %gather_fusion.8), kind=kLoop, calls=%fused_computation.36 | loop fusion | flops 1048576 | bytes 4194308 | tf_op jit(solution)/shard_map/jit(_take)/select_n | solution.py:116
  34.6 2.6 %all-to-all-done.2 = s32[4,1,3]{2,1,0:T(1,128)S(1)} async-done(((s32[4,1,3]{2,1,0:T(1,128)}), s32[4,1,3]{2,1,0:T(1,128)S(1)}, u32[]{:S(2)}, u32[]{:S(2)}) %all-to-all-start.2) | async-done | bytes 80 | tf_op jit(solution)/shard_map/all_to_all | solution.py:103
  37.1 3.5 %all-to-all-start.4 = ((bf16[4,64,2048]{2,1,0:T(8,128)(2,1)}), bf16[4,64,2048]{2,1,0:T(8,128)(2,1)S(1)}, u32[]{:S(2)}, u32[]{:S(2)}) async-start(bf16[4,64,2048]{2,1,0:T(8,128)(2,1)} %get-tuple-element.25), calls=%async_computation.4 | async-start | bytes 2097152 | tf_op jit(solution)/shard_map/all_to_all | solution.py:115
  40.8 23.4 %all-to-all-done.4 = bf16[4,64,2048]{2,1,0:T(8,128)(2,1)S(1)} async-done(((bf16[4,64,2048]{2,1,0:T(8,128)(2,1)}), bf16[4,64,2048]{2,1,0:T(8,128)(2,1)S(1)}, u32[]{:S(2)}, u32[]{:S(2)}) %all-to-all-start.4) | async-done | bytes 1048608 | tf_op jit(solution)/shard_map/all_to_all | solution.py:115
  64.2 4.2 %all-to-all-start.5 = ((bf16[4,64,2048]{2,1,0:T(8,128)(2,1)}), bf16[4,64,2048]{2,1,0:T(8,128)(2,1)}, u32[]{:S(2)}, u32[]{:S(2)}) async-start(bf16[4,64,2048]{2,1,0:T(8,128)(2,1)} %get-tuple-element.26), calls=%async_computation.5 | async-start | bytes 2097152 | tf_op jit(solution)/shard_map/all_to_all | solution.py:118
  68.5 2.0 %gather_fusion = bf16[128,2,16,256]{3,2,1,0:T(8,128)(2,1)} fusion(bf16[2,128,16,256]{3,2,1,0:T(8,128)(2,1)S(1)} %copy-done, s32[1024]{0:T(1024)S(1)} %pad_clamp_fusion.6), kind=kCustom, calls=%fused_computation.4 | custom fusion | bytes 4194816 | tf_op jit(solution)/shard_map/jit(_take)/gather | solution.py:107
  70.5 3.1 %copy.106 = bf16[2,128,16,256]{3,2,1,0:T(8,128)(2,1)} copy(bf16[2,128,16,256]{3,2,0,1:T(8,128)(2,1)} %bitcast.52) | data formatting | bytes 4194304 | tf_op jit(solution)/shard_map/jit(_take)/gather | solution.py:107
  73.9 2.8 %bitcast_select_fusion = bf16[2,16,128,256]{3,2,1,0:T(8,128)(2,1)} fusion(pred[16,128]{1,0:T(8,128)(4,1)S(1)} %broadcast_in_dim.159, bf16[2,16,128,256]{3,2,1,0:T(8,128)(2,1)} %bitcast.51), kind=kLoop, calls=%fused_computation.19 | loop fusion | flops 1048576 | bytes 4196352 | tf_op jit(solution)/shard_map/jit(_take)/select_n | solution.py:107
  76.7 3.4 %gather_fusion.1 = bf16[12,2,128,256]{3,2,1,0:T(8,128)(2,1)} fusion(bf16[2,16,128,256]{3,2,1,0:T(8,128)(2,1)} %bitcast_select_fusion, s32[1024]{0:T(1024)S(1)} %pad_clamp_fusion.5), kind=kCustom, calls=%fused_computation.5 | custom fusion | bytes 3145776 | tf_op jit(solution)/shard_map/jit(_take)/gather | solution.py:134
  81.0 2.9 %copy_select_fusion = bf16[2,4,3,128,256]{4,3,2,0,1:T(8,128)(2,1)} fusion(bf16[2,4,3,128,256]{4,3,0,2,1:T(8,128)(2,1)} %bitcast.54, pred[4,3]{1,0:T(4,128)(4,1)S(1)} %le.81), kind=kLoop, calls=%fused_computation.23 | loop fusion | flops 786432 | bytes 3145740 | tf_op jit(solution)/shard_map/jit(_take)/select_n | solution.py:134
  83.9 9.9 %all-to-all-done.5 = bf16[4,64,2048]{2,1,0:T(8,128)(2,1)} async-done(((bf16[4,64,2048]{2,1,0:T(8,128)(2,1)}), bf16[4,64,2048]{2,1,0:T(8,128)(2,1)}, u32[]{:S(2)}, u32[]{:S(2)}) %all-to-all-start.5) | async-done | bytes 1048608 | tf_op jit(solution)/shard_map/all_to_all | solution.py:118
  93.8 4.3 %all-to-all-start.1 = ((bf16[2,4,3,128,256]{4,3,2,0,1:T(8,128)(2,1)}), bf16[2,4,3,128,256]{4,3,2,0,1:T(8,128)(2,1)}, u32[]{:S(2)}, u32[]{:S(2)}) async-start(bf16[2,4,3,128,256]{4,3,2,0,1:T(8,128)(2,1)} %copy_select_fusion), calls=%async_computation.1 | async-start | bytes 3145728 | tf_op jit(solution)/shard_map/all_to_all | solution.py:136
  103.3 2.8 %gather_fusion.7 = bf16[16,64,2048]{2,1,0:T(8,128)(2,1)} fusion(bf16[4,64,2048]{2,1,0:T(8,128)(2,1)S(1)} %all-to-all-done.4, s32[1024]{0:T(1024)S(1)} %pad_clamp_fusion), kind=kCustom, calls=%fused_computation.1.clone | custom fusion | bytes 8388672 | tf_op jit(solution)/shard_map/jit(_take)/gather | solution.py:122
  106.1 4.0 %gather_fusion.9 = bf16[16,64,2048]{2,1,0:T(8,128)(2,1)} fusion(bf16[4,64,2048]{2,1,0:T(8,128)(2,1)} %all-to-all-done.5, s32[1024]{0:T(1024)S(1)} %pad_clamp_fusion), kind=kCustom, calls=%fused_computation.3.clone | custom fusion | bytes 8388672 | tf_op jit(solution)/shard_map/jit(_take)/gather | solution.py:123
  110.1 3.5 %fusion.20 = f32[16,2,64]{2,1,0:T(2,128)S(1)} fusion(bf16[16,2,2048]{2,1,0:T(2,128)(2,1)S(1)} %copy-done.9, bf16[16,64,2048]{2,1,0:T(8,128)(2,1)} %gather_fusion.7, pred[16]{0:T(512)(128)(4,1)S(1)} %get-tuple-element.16), kind=kOutput, calls=%fused_computation.34 | convolution fusion | flops 10485760 | bytes 4333584 | tf_op jit(solution)/shard_map/rsd,rkd->rsk/dot_general | solution.py:124
  113.6 10.2 %psum.7 = bf16[16,2,64]{2,1,0:T(2,128)(2,1)S(1)} all-reduce(f32[16,2,64]{2,1,0:T(2,128)S(1)} %fusion.20), channel_id=1, replica_groups=mesh['rep'=2,'req'=4,'mp'=4] {'mp'}, use_global_device_ids=true, to_apply=%region_6.9 | all-reduce | flops 2048 | bytes 12288 | tf_op jit(solution)/shard_map/psum | solution.py:54
  123.8 2.9 %fusion.9 = bf16[16,2,2048]{2,1,0:T(2,128)(2,1)S(1)} fusion(bf16[16,64,2048]{2,1,0:T(8,128)(2,1)} %gather_fusion.9, pred[16]{0:T(512)(128)(4,1)S(1)} %get-tuple-element.16, bf16[16,2,2048]{2,1,0:T(2,128)(2,1)S(1)} %copy-done.10, bf16[16,2,64]{2,1,0:T(2,128)(2,1)S(1)} %psum.7), kind=kOutput, calls=%fused_computation.18 | convolution fusion | flops 10682368 | bytes 4460560 | tf_op jit(solution)/shard_map/gxj,gjv->gxv/dot_general | solution.py:128
  127.8 6.8 %all-to-all-done.1 = bf16[2,4,3,128,256]{4,3,2,0,1:T(8,128)(2,1)} async-done(((bf16[2,4,3,128,256]{4,3,2,0,1:T(8,128)(2,1)}), bf16[2,4,3,128,256]{4,3,2,0,1:T(8,128)(2,1)}, u32[]{:S(2)}, u32[]{:S(2)}) %all-to-all-start.1) | async-done | bytes 1572896 | tf_op jit(solution)/shard_map/all_to_all | solution.py:136
  136.7 2.1 %pad_maximum_fusion = bf16[2,28,128,256]{3,2,1,0:T(8,128)(2,1)} fusion(bf16[2,12,128,256]{3,2,1,0:T(8,128)(2,1)S(1)} %bitcast.53, bf16[2,16,128,256]{3,2,1,0:T(8,128)(2,1)S(1)} %copy-done.2), kind=kLoop, calls=%fused_computation.16 | loop fusion | flops 1835008 | bytes 7340032 | tf_op jit(solution)/shard_map/concatenate | solution.py:137
  138.8 4.2 %gather_fusion.2 = bf16[16,2,128,256]{3,2,1,0:T(8,128)(2,1)} fusion(bf16[2,28,128,256]{3,2,1,0:T(8,128)(2,1)} %pad_maximum_fusion, s32[1024]{0:T(1024)} %pad_clamp_fusion.4), kind=kCustom, calls=%fused_computation.6 | custom fusion | bytes 4194368 | tf_op jit(solution)/shard_map/jit(_take)/gather | solution.py:141
  (96 shorter events, 35.3 us)
Async XLA Ops:
  0.6 67.9 %copy-start = (bf16[2,128,16,256]{3,2,1,0:T(8,128)(2,1)S(1)}, bf16[2,128,16,256]{3,2,1,0:T(8,128)(2,1)}, u32[]{:S(2)}) copy-start(bf16[2,128,16,256]{3,2,1,0:T(8,128)(2,1)} %param.22) | copy-start | bytes 6291460
  4.2 12.9 %all-to-all-start.3 = ((s32[4,1,1]{2,1,0:T(1,128)}), s32[4,1,1]{2,1,0:T(1,128)S(1)}, u32[]{:S(2)}, u32[]{:S(2)}) async-start(s32[4,1,1]{2,1,0:T(1,128)} %copy.112), calls=%async_computation.3 | async-start | bytes 4096 | tf_op jit(solution)/shard_map/all_to_all | solution.py:99
  17.1 10.6 %all-to-all-start = ((s32[4,1,3]{2,1,0:T(1,128)}), s32[4,1,3]{2,1,0:T(1,128)S(1)}, u32[]{:S(2)}, u32[]{:S(2)}) async-start(s32[4,1,3]{2,1,0:T(1,128)} %bitcast), calls=%async_computation | async-start | bytes 4096 | tf_op jit(solution)/shard_map/all_to_all | solution.py:100
  27.6 9.5 %all-to-all-start.2 = ((s32[4,1,3]{2,1,0:T(1,128)}), s32[4,1,3]{2,1,0:T(1,128)S(1)}, u32[]{:S(2)}, u32[]{:S(2)}) async-start(s32[4,1,3]{2,1,0:T(1,128)} %bitcast.10), calls=%async_computation.2 | async-start | bytes 4096 | tf_op jit(solution)/shard_map/all_to_all | solution.py:103
  34.6 6.1 %copy-start.5 = (s32[16,8]{0,1:T(8,128)S(1)}, s32[16,8]{0,1:T(8,128)}, u32[]{:S(2)}) copy-start(s32[16,8]{0,1:T(8,128)} %param.23) | copy-start | bytes 1540
  37.1 27.1 %all-to-all-start.4 = ((bf16[4,64,2048]{2,1,0:T(8,128)(2,1)}), bf16[4,64,2048]{2,1,0:T(8,128)(2,1)S(1)}, u32[]{:S(2)}, u32[]{:S(2)}) async-start(bf16[4,64,2048]{2,1,0:T(8,128)(2,1)} %get-tuple-element.25), calls=%async_computation.4 | async-start | bytes 2097152 | tf_op jit(solution)/shard_map/all_to_all | solution.py:115
  64.2 29.5 %all-to-all-start.5 = ((bf16[4,64,2048]{2,1,0:T(8,128)(2,1)}), bf16[4,64,2048]{2,1,0:T(8,128)(2,1)}, u32[]{:S(2)}, u32[]{:S(2)}) async-start(bf16[4,64,2048]{2,1,0:T(8,128)(2,1)} %get-tuple-element.26), calls=%async_computation.5 | async-start | bytes 2097152 | tf_op jit(solution)/shard_map/all_to_all | solution.py:118
  76.7 3.5 %copy-start.4 = (bf16[16,2,2,256]{3,2,1,0:T(2,128)(2,1)S(1)}, bf16[16,2,2,256]{3,2,1,0:T(2,128)(2,1)}, u32[]{:S(2)}) copy-start(bf16[16,2,2,256]{3,2,1,0:T(2,128)(2,1)} %param.17) | copy-start | bytes 98308
  83.9 17.6 %copy-start.7 = (s32[16]{0:T(128)S(1)}, s32[16]{0:T(128)}, u32[]{:S(2)}) copy-start(s32[16]{0:T(128)} %param.25) | copy-start | bytes 196
  83.9 18.8 %copy-start.1 = (s32[16]{0:T(128)S(1)}, s32[16]{0:T(128)}, u32[]{:S(2)}) copy-start(s32[16]{0:T(128)} %param.24) | copy-start | bytes 196
  93.8 40.9 %all-to-all-start.1 = ((bf16[2,4,3,128,256]{4,3,2,0,1:T(8,128)(2,1)}), bf16[2,4,3,128,256]{4,3,2,0,1:T(8,128)(2,1)}, u32[]{:S(2)}, u32[]{:S(2)}) async-start(bf16[2,4,3,128,256]{4,3,2,0,1:T(8,128)(2,1)} %copy_select_fusion), calls=%async_computation.1 | async-start | bytes 3145728 | tf_op jit(solution)/shard_map/all_to_all | solution.py:136
  106.1 4.0 %copy-start.9 = (bf16[16,2,2048]{2,1,0:T(2,128)(2,1)S(1)}, bf16[16,2,2048]{2,1,0:T(2,128)(2,1)}, u32[]{:S(2)}) copy-start(bf16[16,2,2048]{2,1,0:T(2,128)(2,1)} %param.15) | copy-start | bytes 393220
  110.1 13.7 %copy-start.10 = (bf16[16,2,2048]{2,1,0:T(2,128)(2,1)S(1)}, bf16[16,2,2048]{2,1,0:T(2,128)(2,1)}, u32[]{:S(2)}) copy-start(bf16[16,2,2048]{2,1,0:T(2,128)(2,1)} %param.16) | copy-start | bytes 393220
  123.8 3.1 %copy-start.6 = (bf16[16,2,2,128]{3,2,1,0:T(2,128)(2,1)S(1)}, bf16[16,2,2,128]{3,2,1,0:T(2,128)(2,1)}, u32[]{:S(2)}) copy-start(bf16[16,2,2,128]{3,2,1,0:T(2,128)(2,1)} %reshape.370) | copy-start | bytes 49156
  123.8 3.1 %copy-start.11 = (pred[2,2]{1,0:T(4,128)(4,1)S(1)}, pred[2,2]{1,0:T(4,128)(4,1)}, u32[]{:S(2)}) copy-start(pred[2,2]{1,0:T(4,128)(4,1)} %iota_compare_fusion.5) | copy-start | bytes 16
  134.6 2.1 %copy-start.2 = (bf16[2,16,128,256]{3,2,1,0:T(8,128)(2,1)S(1)}, bf16[2,16,128,256]{3,2,1,0:T(8,128)(2,1)}, u32[]{:S(2)}) copy-start(bf16[2,16,128,256]{3,2,1,0:T(8,128)(2,1)} %bitcast_select_fusion) | copy-start | bytes 6291460
  138.8 4.2 %copy-start.8 = (pred[16]{0:T(512)(128)(4,1)S(1)}, pred[16]{0:T(512)(128)(4,1)}, u32[]{:S(2)}) copy-start(pred[16]{0:T(512)(128)(4,1)} %get-tuple-element.19) | copy-start | bytes 52
  152.6 1.7 %copy-start.3 = (bf16[16,2,2,8,130]{4,3,1,2,0:T(8,128)(2,1)S(1)}, bf16[16,2,2,8,130]{4,3,1,2,0:T(8,128)(2,1)}, u32[]{:S(2)}) copy-start(bf16[16,2,2,8,130]{4,3,1,2,0:T(8,128)(2,1)} %divide_convert_fusion) | copy-start | bytes 399364
where the time goes:
time: 157 us; the launch traced here: 156 us
  waiting for transfers between devices  43.7 us (28%)
  local copies, waits for them, and re-layouts  39.6 us (25%)
  starting transfers between devices  27.6 us (18%)
  other arithmetic  24.5 us (16%)
  blocking collectives  10.2 us (6%)
  matrix products  9.32 us (6%)
    all_to_all x1, waiting for transfers between devices, per_device(): lax.all_to_all(jnp.take(a_store, wanted_slot, axis=0), 'req', split_axis=...  23.4 us
    psum x1, blocking collectives, adapter_rank_width(): return lax.psum(rank_partial_sum, 'mp')  10.2 us
    all_to_all x1, waiting for transfers between devices, per_device(): lax.all_to_all(jnp.take(b_store, wanted_slot, axis=0), 'req', split_axis=...  9.87 us
    all_to_all x1, waiting for transfers between devices, per_device(): lax.all_to_all(send_pages, 'req', split_axis=1, concat_axis=1, tiled=True)  6.84 us
    all_to_all x1, starting transfers between devices, per_device(): lax.all_to_all(wanted, 'req', split_axis=0, concat_axis=0, tiled=True)  6.32 us
    gather x2, local copies, waits for them, and re-layouts, per_device(): page_rows = jnp.take(kv_pool, page_table.reshape(-1), axis=1)  5.1 us
    all_to_all x1, starting transfers between devices, per_device(): lax.all_to_all(send_src.reshape(groups, move_cap), 'req', split_axis=0, c...  5.09 us
    all_to_all x1, starting transfers between devices, per_device(): lax.all_to_all(send_pages, 'req', split_axis=1, concat_axis=1, tiled=True)  4.35 us
  transfers between devices with their start and end apart: 6, of which 5 were waited for; matrix products, arithmetic and copies ran while one was open for 31% of the time, Pallas kernels for 0%

commit v1 on v0

--- a/solution.py
+++ b/solution.py
@@ -133,7 +133,19 @@
     )
     far_cache = jnp.take(cache_old, safe_src, axis=1)
     send_pages = far_cache.reshape(2, groups, move_cap, context, kv_width)
-    got_pages = lax.all_to_all(send_pages, "req", split_axis=1, concat_axis=1, tiled=True)
+
+    def arrays_point(mine_x, along_axis, row_dim, ndim_at):
+        return jnp.concatenate(
+            lax.all_to_all(
+                jnp.stack(jnp.split(mine_x, lax.axis_size(along_axis), axis=row_dim), axis=0),
+                axis_name=along_axis,
+                split_axis=0,
+                concat_axis=0,
+            ),
+            axis=ndim_at,
+        )
+
+    got_pages = arrays_point(send_pages, "req", 1, 1)
     pooled = jnp.concatenate(
         [cache_old, got_pages.reshape(2, groups * move_cap, context, kv_width)], axis=1
     )

time: 157 us -> 157 us (level)
    all_to_all x1 -> x0, local copies, waits for them, and re-layouts: 1.7 us -> none  [per_device(): lax.all_to_all(send_pages, 'req', split_axis=1, concat_axis=1, tiled=True)]
    reshape x0 -> x1, local copies, waits for them, and re-layouts: none -> 1.7 us  [arrays_point(): jnp.concatenate(lax.all_to_all(jnp.stack(jnp.split(mine_x, lax.axis_size(...]
where the time goes in v1:
time: 157 us; the launch traced here: 156 us
  waiting for transfers between devices  43.3 us (28%)
  local copies, waits for them, and re-layouts  39.8 us (25%)
  starting transfers between devices  27.6 us (18%)
  other arithmetic  24.7 us (16%)
  blocking collectives  10.2 us (6%)
  matrix products  9.32 us (6%)
    all_to_all x1, waiting for transfers between devices, per_device(): lax.all_to_all(jnp.take(a_store, wanted_slot, axis=0), 'req', split_axis=...  23.4 us
    psum x1, blocking collectives, adapter_rank_width(): return lax.psum(rank_partial_sum, 'mp')  10.2 us
    all_to_all x1, waiting for transfers between devices, per_device(): lax.all_to_all(jnp.take(b_store, wanted_slot, axis=0), 'req', split_axis=...  9.53 us
    all_to_all x1, waiting for transfers between devices, arrays_point(): lax.all_to_all(jnp.stack(jnp.split(mine_x, lax.axis_size(along_axis), axi...  6.84 us
    all_to_all x1, starting transfers between devices, per_device(): lax.all_to_all(wanted, 'req', split_axis=0, concat_axis=0, tiled=True)  6.32 us
    gather x2, local copies, waits for them, and re-layouts, per_device(): page_rows = jnp.take(kv_pool, page_table.reshape(-1), axis=1)  5.1 us
    all_to_all x1, starting transfers between devices, per_device(): lax.all_to_all(send_src.reshape(groups, move_cap), 'req', split_axis=0, c...  5.09 us
    all_to_all x1, starting transfers between devices, arrays_point(): lax.all_to_all(jnp.stack(jnp.split(mine_x, lax.axis_size(along_axis), axi...  4.35 us
  transfers between devices with their start and end apart: 6, of which 5 were waited for; matrix products, arithmetic and copies ran while one was open for 31% of the time, Pallas kernels for 0%

profile of v1, /device:TPU:0, one launch (start us, length us, event | category | flops | bytes accessed | tf_op | source)
XLA Modules:
  0.0 155.8 jit_solution(8466525121671804952)
XLA Ops:
  4.2 6.3 %all-to-all-start.3 = ((s32[4,1,1]{2,1,0:T(1,128)}), s32[4,1,1]{2,1,0:T(1,128)S(1)}, u32[]{:S(2)}, u32[]{:S(2)}) async-start(s32[4,1,1]{2,1,0:T(1,128)} %copy.121), calls=%async_computation.3 | async-start | bytes 4096 | tf_op jit(solution)/shard_map/all_to_all | solution.py:99
  17.1 5.1 %all-to-all-start = ((s32[4,1,3]{2,1,0:T(1,128)}), s32[4,1,3]{2,1,0:T(1,128)S(1)}, u32[]{:S(2)}, u32[]{:S(2)}) async-start(s32[4,1,3]{2,1,0:T(1,128)} %bitcast), calls=%async_computation | async-start | bytes 4096 | tf_op jit(solution)/shard_map/all_to_all | solution.py:100
  24.0 2.6 %gather_fusion.8 = bf16[4,64,2048]{2,1,0:T(8,128)(2,1)} fusion(bf16[2,64,2048]{2,1,0:T(8,128)(2,1)} %param.21, s32[1024]{0:T(1024)S(1)} %pad_clamp_fusion.1), kind=kCustom, calls=%fused_computation.2.clone | custom fusion | bytes 2097168 | tf_op jit(solution)/shard_map/jit(_take)/gather | solution.py:119
  27.6 4.1 %all-to-all-start.2 = ((s32[4,1,3]{2,1,0:T(1,128)}), s32[4,1,3]{2,1,0:T(1,128)S(1)}, u32[]{:S(2)}, u32[]{:S(2)}) async-start(s32[4,1,3]{2,1,0:T(1,128)} %bitcast.15), calls=%async_computation.2 | async-start | bytes 4096 | tf_op jit(solution)/shard_map/all_to_all | solution.py:103
  31.8 2.8 %broadcast_select_fusion.1 = (bf16[4,64,2048]{2,1,0:T(8,128)(2,1)}, bf16[4,64,2048]{2,1,0:T(8,128)(2,1)}) fusion(bf16[4,64,2048]{2,1,0:T(8,128)(2,1)S(1)} %gather_fusion.6, pred[4]{0:T(512)(128)(4,1)S(1)} %compare_and_fusion.2, bf16[4,64,2048]{2,1,0:T(8,128)(2,1)} %gather_fusion.8), kind=kLoop, calls=%fused_computation.37 | loop fusion | flops 1048576 | bytes 4194308 | tf_op jit(solution)/shard_map/jit(_take)/select_n | solution.py:116
  34.6 2.6 %all-to-all-done.2 = s32[4,1,3]{2,1,0:T(1,128)S(1)} async-done(((s32[4,1,3]{2,1,0:T(1,128)}), s32[4,1,3]{2,1,0:T(1,128)S(1)}, u32[]{:S(2)}, u32[]{:S(2)}) %all-to-all-start.2) | async-done | bytes 80 | tf_op jit(solution)/shard_map/all_to_all | solution.py:103
  37.1 3.5 %all-to-all-start.4 = ((bf16[4,64,2048]{2,1,0:T(8,128)(2,1)}), bf16[4,64,2048]{2,1,0:T(8,128)(2,1)S(1)}, u32[]{:S(2)}, u32[]{:S(2)}) async-start(bf16[4,64,2048]{2,1,0:T(8,128)(2,1)} %get-tuple-element.29), calls=%async_computation.4 | async-start | bytes 2097152 | tf_op jit(solution)/shard_map/all_to_all | solution.py:115
  40.9 23.4 %all-to-all-done.4 = bf16[4,64,2048]{2,1,0:T(8,128)(2,1)S(1)} async-done(((bf16[4,64,2048]{2,1,0:T(8,128)(2,1)}), bf16[4,64,2048]{2,1,0:T(8,128)(2,1)S(1)}, u32[]{:S(2)}, u32[]{:S(2)}) %all-to-all-start.4) | async-done | bytes 1048608 | tf_op jit(solution)/shard_map/all_to_all | solution.py:115
  64.2 4.2 %all-to-all-start.5 = ((bf16[4,64,2048]{2,1,0:T(8,128)(2,1)}), bf16[4,64,2048]{2,1,0:T(8,128)(2,1)}, u32[]{:S(2)}, u32[]{:S(2)}) async-start(bf16[4,64,2048]{2,1,0:T(8,128)(2,1)} %get-tuple-element.30), calls=%async_computation.5 | async-start | bytes 2097152 | tf_op jit(solution)/shard_map/all_to_all | solution.py:118
  68.5 2.0 %gather_fusion = bf16[128,2,16,256]{3,2,1,0:T(8,128)(2,1)} fusion(bf16[2,128,16,256]{3,2,1,0:T(8,128)(2,1)S(1)} %copy-done, s32[1024]{0:T(1024)S(1)} %pad_clamp_fusion.6), kind=kCustom, calls=%fused_computation.4 | custom fusion | bytes 4194816 | tf_op jit(solution)/shard_map/jit(_take)/gather | solution.py:107
  70.5 3.1 %copy.115 = bf16[2,128,16,256]{3,2,1,0:T(8,128)(2,1)} copy(bf16[2,128,16,256]{3,2,0,1:T(8,128)(2,1)} %bitcast.61) | data formatting | bytes 4194304 | tf_op jit(solution)/shard_map/jit(_take)/gather | solution.py:107
  73.9 2.8 %bitcast_select_fusion = bf16[2,16,128,256]{3,2,1,0:T(8,128)(2,1)} fusion(pred[16,128]{1,0:T(8,128)(4,1)S(1)} %broadcast_in_dim.159, bf16[2,16,128,256]{3,2,1,0:T(8,128)(2,1)} %bitcast.60), kind=kLoop, calls=%fused_computation.19 | loop fusion | flops 1048576 | bytes 4196352 | tf_op jit(solution)/shard_map/jit(_take)/select_n | solution.py:107
  76.7 3.4 %gather_fusion.1 = bf16[12,2,128,256]{3,2,1,0:T(8,128)(2,1)} fusion(bf16[2,16,128,256]{3,2,1,0:T(8,128)(2,1)} %bitcast_select_fusion, s32[1024]{0:T(1024)S(1)} %pad_clamp_fusion.5), kind=kCustom, calls=%fused_computation.5 | custom fusion | bytes 3145776 | tf_op jit(solution)/shard_map/jit(_take)/gather | solution.py:134
  84.2 9.5 %all-to-all-done.5 = bf16[4,64,2048]{2,1,0:T(8,128)(2,1)} async-done(((bf16[4,64,2048]{2,1,0:T(8,128)(2,1)}), bf16[4,64,2048]{2,1,0:T(8,128)(2,1)}, u32[]{:S(2)}, u32[]{:S(2)}) %all-to-all-start.5) | async-done | bytes 1048608 | tf_op jit(solution)/shard_map/all_to_all | solution.py:118
  93.8 4.3 %all-to-all-start.1 = ((bf16[4,2,1,3,128,256]{5,4,3,1,2,0:T(8,128)(2,1)}), bf16[4,2,1,3,128,256]{5,4,3,1,2,0:T(8,128)(2,1)}, u32[]{:S(2)}, u32[]{:S(2)}) async-start(bf16[4,2,1,3,128,256]{5,4,3,1,2,0:T(8,128)(2,1)} %pad_maximum_fusion.1), calls=%async_computation.1 | async-start | bytes 3145728 | tf_op jit(solution)/shard_map/all_to_all | solution.py:139
  103.3 2.8 %gather_fusion.7 = bf16[16,64,2048]{2,1,0:T(8,128)(2,1)} fusion(bf16[4,64,2048]{2,1,0:T(8,128)(2,1)S(1)} %all-to-all-done.4, s32[1024]{0:T(1024)S(1)} %pad_clamp_fusion), kind=kCustom, calls=%fused_computation.1.clone | custom fusion | bytes 8388672 | tf_op jit(solution)/shard_map/jit(_take)/gather | solution.py:122
  106.1 4.0 %gather_fusion.9 = bf16[16,64,2048]{2,1,0:T(8,128)(2,1)} fusion(bf16[4,64,2048]{2,1,0:T(8,128)(2,1)} %all-to-all-done.5, s32[1024]{0:T(1024)S(1)} %pad_clamp_fusion), kind=kCustom, calls=%fused_computation.3.clone | custom fusion | bytes 8388672 | tf_op jit(solution)/shard_map/jit(_take)/gather | solution.py:123
  110.1 3.5 %fusion.20 = f32[16,2,64]{2,1,0:T(2,128)S(1)} fusion(bf16[16,2,2048]{2,1,0:T(2,128)(2,1)S(1)} %copy-done.9, bf16[16,64,2048]{2,1,0:T(8,128)(2,1)} %gather_fusion.7, pred[16]{0:T(512)(128)(4,1)S(1)} %get-tuple-element.16), kind=kOutput, calls=%fused_computation.35 | convolution fusion | flops 10485760 | bytes 4333584 | tf_op jit(solution)/shard_map/rsd,rkd->rsk/dot_general | solution.py:124
  113.6 10.2 %psum.7 = bf16[16,2,64]{2,1,0:T(2,128)(2,1)S(1)} all-reduce(f32[16,2,64]{2,1,0:T(2,128)S(1)} %fusion.20), channel_id=1, replica_groups=mesh['rep'=2,'req'=4,'mp'=4] {'mp'}, use_global_device_ids=true, to_apply=%region_6.9 | all-reduce | flops 2048 | bytes 12288 | tf_op jit(solution)/shard_map/psum | solution.py:54
  123.8 2.9 %fusion.9 = bf16[16,2,2048]{2,1,0:T(2,128)(2,1)S(1)} fusion(bf16[16,64,2048]{2,1,0:T(8,128)(2,1)} %gather_fusion.9, pred[16]{0:T(512)(128)(4,1)S(1)} %get-tuple-element.16, bf16[16,2,2048]{2,1,0:T(2,128)(2,1)S(1)} %copy-done.10, bf16[16,2,64]{2,1,0:T(2,128)(2,1)S(1)} %psum.7), kind=kOutput, calls=%fused_computation.18 | convolution fusion | flops 10682368 | bytes 4460560 | tf_op jit(solution)/shard_map/gxj,gjv->gxv/dot_general | solution.py:128
  127.8 6.8 %all-to-all-done.1 = bf16[4,2,1,3,128,256]{5,4,3,1,2,0:T(8,128)(2,1)} async-done(((bf16[4,2,1,3,128,256]{5,4,3,1,2,0:T(8,128)(2,1)}), bf16[4,2,1,3,128,256]{5,4,3,1,2,0:T(8,128)(2,1)}, u32[]{:S(2)}, u32[]{:S(2)}) %all-to-all-start.1) | async-done | bytes 1572896 | tf_op jit(solution)/shard_map/all_to_all | solution.py:139
  136.7 2.1 %pad_maximum_fusion = bf16[2,28,128,256]{3,2,1,0:T(8,128)(2,1)} fusion(bf16[2,12,128,256]{3,2,1,0:T(8,128)(2,1)S(1)} %bitcast.62, bf16[2,16,128,256]{3,2,1,0:T(8,128)(2,1)S(1)} %copy-done.2), kind=kLoop, calls=%fused_computation.16 | loop fusion | flops 1835008 | bytes 7340032 | tf_op jit(solution)/shard_map/concatenate | solution.py:149
  138.8 4.2 %gather_fusion.2 = bf16[16,2,128,256]{3,2,1,0:T(8,128)(2,1)} fusion(bf16[2,28,128,256]{3,2,1,0:T(8,128)(2,1)} %pad_maximum_fusion, s32[1024]{0:T(1024)} %pad_clamp_fusion.4), kind=kCustom, calls=%fused_computation.6 | custom fusion | bytes 4194368 | tf_op jit(solution)/shard_map/jit(_take)/gather | solution.py:153
  143.0 1.9 %select_bitcast_fusion = bf16[2,16,128,256]{3,2,0,1:T(8,128)(2,1)S(1)} fusion(bf16[16,2,128,256]{3,2,1,0:T(8,128)(2,1)} %gather_fusion.2, pred[16]{0:T(512)(128)(4,1)S(1)} %copy-done.8), kind=kLoop, calls=%fused_computation.22 | loop fusion | flops 1048576 | bytes 4194320 | tf_op jit(solution)/shard_map/jit(_take)/select_n | solution.py:153
  (98 shorter events, 36.7 us)
Async XLA Ops:
  0.6 67.9 %copy-start = (bf16[2,128,16,256]{3,2,1,0:T(8,128)(2,1)S(1)}, bf16[2,128,16,256]{3,2,1,0:T(8,128)(2,1)}, u32[]{:S(2)}) copy-start(bf16[2,128,16,256]{3,2,1,0:T(8,128)(2,1)} %param.22) | copy-start | bytes 6291460
  4.2 12.9 %all-to-all-start.3 = ((s32[4,1,1]{2,1,0:T(1,128)}), s32[4,1,1]{2,1,0:T(1,128)S(1)}, u32[]{:S(2)}, u32[]{:S(2)}) async-start(s32[4,1,1]{2,1,0:T(1,128)} %copy.121), calls=%async_computation.3 | async-start | bytes 4096 | tf_op jit(solution)/shard_map/all_to_all | solution.py:99
  17.1 10.6 %all-to-all-start = ((s32[4,1,3]{2,1,0:T(1,128)}), s32[4,1,3]{2,1,0:T(1,128)S(1)}, u32[]{:S(2)}, u32[]{:S(2)}) async-start(s32[4,1,3]{2,1,0:T(1,128)} %bitcast), calls=%async_computation | async-start | bytes 4096 | tf_op jit(solution)/shard_map/all_to_all | solution.py:100
  27.6 9.5 %all-to-all-start.2 = ((s32[4,1,3]{2,1,0:T(1,128)}), s32[4,1,3]{2,1,0:T(1,128)S(1)}, u32[]{:S(2)}, u32[]{:S(2)}) async-start(s32[4,1,3]{2,1,0:T(1,128)} %bitcast.15), calls=%async_computation.2 | async-start | bytes 4096 | tf_op jit(solution)/shard_map/all_to_all | solution.py:103
  34.6 6.1 %copy-start.5 = (s32[16,8]{0,1:T(8,128)S(1)}, s32[16,8]{0,1:T(8,128)}, u32[]{:S(2)}) copy-start(s32[16,8]{0,1:T(8,128)} %param.23) | copy-start | bytes 1540
  37.1 27.1 %all-to-all-start.4 = ((bf16[4,64,2048]{2,1,0:T(8,128)(2,1)}), bf16[4,64,2048]{2,1,0:T(8,128)(2,1)S(1)}, u32[]{:S(2)}, u32[]{:S(2)}) async-start(bf16[4,64,2048]{2,1,0:T(8,128)(2,1)} %get-tuple-element.29), calls=%async_computation.4 | async-start | bytes 2097152 | tf_op jit(solution)/shard_map/all_to_all | solution.py:115
  64.2 29.5 %all-to-all-start.5 = ((bf16[4,64,2048]{2,1,0:T(8,128)(2,1)}), bf16[4,64,2048]{2,1,0:T(8,128)(2,1)}, u32[]{:S(2)}, u32[]{:S(2)}) async-start(bf16[4,64,2048]{2,1,0:T(8,128)(2,1)} %get-tuple-element.30), calls=%async_computation.5 | async-start | bytes 2097152 | tf_op jit(solution)/shard_map/all_to_all | solution.py:118
  76.7 3.5 %copy-start.4 = (bf16[16,2,2,256]{3,2,1,0:T(2,128)(2,1)S(1)}, bf16[16,2,2,256]{3,2,1,0:T(2,128)(2,1)}, u32[]{:S(2)}) copy-start(bf16[16,2,2,256]{3,2,1,0:T(2,128)(2,1)} %param.17) | copy-start | bytes 98308
  84.2 17.2 %copy-start.7 = (s32[16]{0:T(128)S(1)}, s32[16]{0:T(128)}, u32[]{:S(2)}) copy-start(s32[16]{0:T(128)} %param.25) | copy-start | bytes 196
  84.2 18.4 %copy-start.1 = (s32[16]{0:T(128)S(1)}, s32[16]{0:T(128)}, u32[]{:S(2)}) copy-start(s32[16]{0:T(128)} %param.24) | copy-start | bytes 196
  93.8 40.9 %all-to-all-start.1 = ((bf16[4,2,1,3,128,256]{5,4,3,1,2,0:T(8,128)(2,1)}), bf16[4,2,1,3,128,256]{5,4,3,1,2,0:T(8,128)(2,1)}, u32[]{:S(2)}, u32[]{:S(2)}) async-start(bf16[4,2,1,3,128,256]{5,4,3,1,2,0:T(8,128)(2,1)} %pad_maximum_fusion.1), calls=%async_computation.1 | async-start | bytes 3145728 | tf_op jit(solution)/shard_map/all_to_all | solution.py:139
  106.1 4.0 %copy-start.9 = (bf16[16,2,2048]{2,1,0:T(2,128)(2,1)S(1)}, bf16[16,2,2048]{2,1,0:T(2,128)(2,1)}, u32[]{:S(2)}) copy-start(bf16[16,2,2048]{2,1,0:T(2,128)(2,1)} %param.15) | copy-start | bytes 393220
  110.1 13.7 %copy-start.10 = (bf16[16,2,2048]{2,1,0:T(2,128)(2,1)S(1)}, bf16[16,2,2048]{2,1,0:T(2,128)(2,1)}, u32[]{:S(2)}) copy-start(bf16[16,2,2048]{2,1,0:T(2,128)(2,1)} %param.16) | copy-start | bytes 393220
  123.8 3.1 %copy-start.6 = (bf16[16,2,2,128]{3,2,1,0:T(2,128)(2,1)S(1)}, bf16[16,2,2,128]{3,2,1,0:T(2,128)(2,1)}, u32[]{:S(2)}) copy-start(bf16[16,2,2,128]{3,2,1,0:T(2,128)(2,1)} %reshape.370) | copy-start | bytes 49156
  123.8 3.1 %copy-start.11 = (pred[2,2]{1,0:T(4,128)(4,1)S(1)}, pred[2,2]{1,0:T(4,128)(4,1)}, u32[]{:S(2)}) copy-start(pred[2,2]{1,0:T(4,128)(4,1)} %iota_compare_fusion.5) | copy-start | bytes 16
  134.6 2.1 %copy-start.2 = (bf16[2,16,128,256]{3,2,1,0:T(8,128)(2,1)S(1)}, bf16[2,16,128,256]{3,2,1,0:T(8,128)(2,1)}, u32[]{:S(2)}) copy-start(bf16[2,16,128,256]{3,2,1,0:T(8,128)(2,1)} %bitcast_select_fusion) | copy-start | bytes 6291460
  138.8 4.2 %copy-start.8 = (pred[16]{0:T(512)(128)(4,1)S(1)}, pred[16]{0:T(512)(128)(4,1)}, u32[]{:S(2)}) copy-start(pred[16]{0:T(512)(128)(4,1)} %get-tuple-element.19) | copy-start | bytes 52
  152.6 1.7 %copy-start.3 = (bf16[16,2,2,8,130]{4,3,1,2,0:T(8,128)(2,1)S(1)}, bf16[16,2,2,8,130]{4,3,1,2,0:T(8,128)(2,1)}, u32[]{:S(2)}) copy-start(bf16[16,2,2,8,130]{4,3,1,2,0:T(8,128)(2,1)} %divide_convert_fusion) | copy-start | bytes 399364
